TPU v7x, 32 devices: a whole 2x2x4 slice. The times are simulated.
32 devices in a mesh: dp: 4 (over z), seq: 8 (over y, x, core).
Axes of the slice: x: 2, y: 2, z: 4, core: 2. Of those that a mesh axis runs over, the one named last changes fastest.
Arguments:
- tiles: bfloat16 [4, 1536, 768], P('dp', 'seq'), may hold values from -40 to 40
- cotangent: bfloat16 [4, 1536, 768], P('dp', 'seq'), may hold values from -0.078125 to 0.078125
- segment_of: int32 [4, 1536, 1], P('dp', 'seq'), may hold values from 0 to 15; in each aligned block of 192 rows (0 to 191, 192 to 383, ..., all dimensions but the last counted through in order) at most 20 rows name the same one
- tissue_count: int32 [4], P('dp'), may hold values from 768 to 1536
- w_query: bfloat16 [768, 768], P('seq'), may hold values from -0.21875 to 0.21875
- w_key: bfloat16 [768, 768], P('seq'), may hold values from -0.21875 to 0.21875
- w_value: bfloat16 [768, 768], P('seq'), may hold values from -0.21875 to 0.21875
- w_out: bfloat16 [768, 768], P('seq'), may hold values from -2.390625 to 2.390625
Outputs:
- layer_out: bfloat16 [4, 1536, 768], P('dp', 'seq')
- grad_value: float32 [768, 768], P('seq')
Inputs may be any that keep to these rules, and one draw needn't show every extreme that they name: `segment_of`: within one slide, the 192 tiles of one block name one group at most 20 times; some group is named exactly 20 times.
All inputs are finite; a program needn't handle non-finite values.
Results may differ from a plain program's by a relative error of at most 0.014.
Values may be sent and summed in bfloat16 or wider, within the bound.
No kernel may reach another device: no remote copies, remote signals or barrier semaphores. Data moves between devices by JAX's collectives and lax.ppermute only.
A program may use at most 64 MiB of HBM per device.

v0:
```python
import jax
import jax.numpy as jnp
from jax import lax
from jax.sharding import PartitionSpec as P

HEADS = 12
SEG_DEV = 2
NEG_BIG = -1e30


def contract_last(left, right):
    return lax.dot_general(
        left, right, (((1,), (1,)), ((), ())), preferred_element_type=jnp.float32
    )


def contract_first(left, right):
    return lax.dot_general(
        left, right, (((0,), (0,)), ((), ())), preferred_element_type=jnp.float32
    )


def local(tiles, cotangent, segment_of, tissue_count, w_query, w_key, w_value, w_out):
    rows = tiles.shape[1]
    width = tiles.shape[2]
    heads = HEADS
    head_dim = width // heads
    scale = head_dim ** (-0.5)
    seq_count = lax.axis_size("seq")
    own_index = lax.axis_index("seq")
    segments = SEG_DEV * seq_count
    capacity = 5 * rows // (3 * segments)
    slots = segments * capacity
    per_segment = seq_count * capacity
    full_query, full_key, full_value, full_out = (
        lax.all_gather(w_query, "seq", axis=0, tiled=True),
        lax.all_gather(w_key, "seq", axis=0, tiled=True),
        lax.all_gather(w_value, "seq", axis=0, tiled=True),
        lax.all_gather(w_out, "seq", axis=0, tiled=True),
    )
    inputs = tiles[0]
    position = own_index * rows + jnp.arange(rows, dtype=jnp.int32)
    inside = position < tissue_count[0]
    masked_cot = cotangent[0] * inside[:, None].astype(jnp.bfloat16)
    query_rows = jnp.dot(inputs, full_query, preferred_element_type=jnp.float32).astype(
        jnp.bfloat16
    )
    key_rows = jnp.dot(inputs, full_key, preferred_element_type=jnp.float32).astype(jnp.bfloat16)
    value_rows = jnp.dot(inputs, full_value, preferred_element_type=jnp.float32).astype(
        jnp.bfloat16
    )
    dout_rows = contract_last(masked_cot, full_out).astype(jnp.bfloat16)

    def by_heads(block):
        return block.reshape(rows, heads, head_dim).transpose(1, 0, 2)

    query_heads = by_heads(query_rows)
    key_heads = by_heads(key_rows)
    visible = inside[None, :] | jnp.eye(rows, dtype=bool)

    def local_scores(query_one, key_one):
        scores = contract_last(query_one, key_one) * scale
        return jnp.where(visible, scores, NEG_BIG)

    def local_stats(pair):
        scores = local_scores(pair[0], pair[1])
        top = jnp.max(scores, axis=1)
        total = jnp.sum(jnp.exp(scores - top[:, None]), axis=1)
        return (top, total)

    local_max, local_sum = lax.map(local_stats, (query_heads, key_heads))
    stats_rows = jnp.stack([local_max.T, local_sum.T], axis=1)
    segment_rows = segment_of[0, :, 0]
    member = (segment_rows[:, None] == jnp.arange(segments, dtype=jnp.int32)[None, :]).astype(
        jnp.int32
    )
    rank = jnp.sum(jnp.cumsum(member, axis=0) * member, axis=1) - 1
    slot_index = segment_rows * capacity + rank
    source_row = (
        jnp.full((slots,), rows, jnp.int32).at[slot_index].set(jnp.arange(rows, dtype=jnp.int32))
    )
    state_rows = jnp.where(inside, 2, 1).astype(jnp.int32)

    def to_slots(block):
        padded = jnp.concatenate([block, jnp.zeros((1,) + block.shape[1:], block.dtype)], axis=0)
        gathered = jnp.take(padded, source_row, axis=0)
        return gathered.reshape((seq_count, SEG_DEV, capacity) + block.shape[1:])

    members = [query_rows, key_rows, value_rows, dout_rows]
    bulk_rows = jnp.stack(members, axis=1)

    def unpack(bulk_one):
        return (bulk_one[:, 0], bulk_one[:, 1], bulk_one[:, 2], bulk_one[:, 3])

    send_bulk = to_slots(bulk_rows)
    send_stats = to_slots(stats_rows)
    send_state = to_slots(state_rows)
    eye_slots = jnp.eye(per_segment, dtype=bool)
    bulk = lax.all_to_all(
        send_bulk.astype(jnp.float32), "seq", split_axis=0, concat_axis=2, tiled=True
    ).astype(send_bulk.dtype)
    stats = lax.all_to_all(send_stats, "seq", split_axis=0, concat_axis=2, tiled=True)
    state = lax.all_to_all(send_state, "seq", split_axis=0, concat_axis=2, tiled=True)

    def one_segment(item):
        bulk_one, stats_one, state_one = item
        query_seg, key_seg, value_seg, dout_seg = unpack(bulk_one)
        slot_count = query_seg.shape[0]
        query_seg = query_seg.reshape(slot_count, heads, head_dim)
        key_seg = key_seg.reshape(slot_count, heads, head_dim)
        value_seg = value_seg.reshape(slot_count, heads, head_dim)
        dout_seg = dout_seg.reshape(slot_count, heads, head_dim)
        seen = (state_one == 2)[None, :] | eye_slots
        scores = (
            jnp.einsum("qhc,khc->hqk", query_seg, key_seg, preferred_element_type=jnp.float32)
            * scale
        )
        scores = jnp.where(seen[None], scores, NEG_BIG)
        far_max = jnp.max(scores, axis=2)
        far_sum = jnp.sum(jnp.exp(scores - far_max[:, :, None]), axis=2)
        seg_near_max = stats_one[:, 0, :].T
        seg_near_sum = stats_one[:, 1, :].T
        top = jnp.maximum(far_max, seg_near_max)
        log_total = top + jnp.log(
            seg_near_sum * jnp.exp(seg_near_max - top) + far_sum * jnp.exp(far_max - top)
        )
        weights = jnp.exp(scores - log_total[:, :, None]).astype(jnp.bfloat16)
        far_out = jnp.einsum("hqk,khc->qhc", weights, value_seg, preferred_element_type=jnp.float32)
        far_grad = jnp.einsum("hqk,qhc->khc", weights, dout_seg, preferred_element_type=jnp.float32)
        far_out = far_out.astype(jnp.bfloat16).reshape(slot_count, width)
        far_grad = far_grad.astype(jnp.bfloat16).reshape(slot_count, width)
        return (far_out, far_grad, log_total.T)

    far_out, far_grad, totals = lax.map(one_segment, (bulk[0], stats[0], state[0]))
    back_bulk = jnp.stack([far_out, far_grad], axis=2)[None]
    back_lse = totals[None]
    home_bulk, home_lse = (
        lax.all_to_all(
            back_bulk.astype(jnp.float32), "seq", split_axis=2, concat_axis=0, tiled=True
        ).astype(back_bulk.dtype),
        lax.all_to_all(back_lse, "seq", split_axis=2, concat_axis=0, tiled=True),
    )
    far_rows = jnp.take(home_bulk.reshape((slots,) + back_bulk.shape[3:]), slot_index, axis=0)
    lse_rows = jnp.take(home_lse.reshape(slots, heads), slot_index, axis=0)

    def local_apply(item):
        query_one, key_one, value_one, dout_one, lse_one = item
        scores = local_scores(query_one, key_one)
        weights = jnp.exp(scores - lse_one[:, None]).astype(jnp.bfloat16)
        near_out = jnp.dot(weights, value_one, preferred_element_type=jnp.float32)
        near_grad = contract_first(weights, dout_one)
        return (near_out, near_grad)

    near_out, near_grad = lax.map(
        local_apply, (query_heads, key_heads, by_heads(value_rows), by_heads(dout_rows), lse_rows.T)
    )
    near_grad = near_grad.transpose(1, 0, 2).reshape(rows, width).astype(jnp.bfloat16)
    far_out_rows = far_rows[:, 0]
    grad_right = far_rows[:, 1]
    attention = (
        near_out.transpose(1, 0, 2).reshape(rows, width) + far_out_rows.astype(jnp.float32)
    ).astype(jnp.bfloat16)
    layer_rows = jnp.dot(attention, full_out, preferred_element_type=jnp.float32).astype(
        jnp.bfloat16
    )
    grad_part = lax.psum_scatter(
        (contract_first(inputs, near_grad) + contract_first(inputs, grad_right)).astype(
            jnp.bfloat16
        ),
        "seq",
        scatter_dimension=0,
        tiled=True,
    ).astype(jnp.float32)
    grad_part = lax.psum(grad_part.astype(jnp.bfloat16), "dp").astype(jnp.float32)
    return (layer_rows[None], grad_part)


def solution(mesh):
    placed = (
        P("dp", "seq", None),
        P("dp", "seq", None),
        P("dp", "seq", None),
        P("dp"),
        P("seq", None),
        P("seq", None),
        P("seq", None),
        P("seq", None),
    )
    return jax.shard_map(
        local,
        mesh=mesh,
        in_specs=placed,
        out_specs=(P("dp", "seq", None), P("seq", None)),
        check_vma=False,
    )
```

profile of v0, /device:TPU:0, one launch (start us, length us, event | category | flops | bytes accessed | tf_op | source)
XLA Modules:
  0.0 328.2 jit_solution(14311517233252371151)
XLA Ops:
  14.5 2.5 gather_fusion.1
  17.6 5.2 %all-to-all-start.1 = ((s32[8,2,20]{2,1,0:T(2,128)}), s32[8,2,20]{2,1,0:T(2,128)S(1)}, u32[]{:S(2)}, u32[]{:S(2)}) async-start(s32[8,2,20]{2,1,0:T(2,128)} %broadcast_select_fusion.2), calls=%async_computation.1 | async-start | bytes 16384 | tf_op jit(solution)/shard_map/all_to_all | solution.py:103
  23.4 13.1 %all-gather.5.cloned.1.call-done = bf16[768,768]{1,0:T(8,128)(2,1)} async-done(((bf16[96,768]{1,0:T(8,128)(2,1)}), bf16[768,768]{1,0:T(8,128)(2,1)}) %all-gather.5.cloned.1.call-update) | async-done | bytes 1179664 | tf_op jit(solution)/shard_map/all_gather | solution.py:36
  38.7 23.7 %all-gather.7.cloned.1.call-done = bf16[768,768]{1,0:T(8,128)(2,1)} async-done(((bf16[96,768]{1,0:T(8,128)(2,1)}), bf16[768,768]{1,0:T(8,128)(2,1)}) %all-gather.7.cloned.1.call-update) | async-done | bytes 1179664 | tf_op jit(solution)/shard_map/all_gather | solution.py:37
  64.5 4.9 %while.41 = (s32[]{:T(128)}, f32[12,192]{1,0:T(8,128)S(1)}, f32[12,192]{1,0:T(8,128)S(1)}, bf16[12,192,64]{2,1,0:T(8,128)(2,1)S(1)}, bf16[12,192,64]{2,1,0:T(8,1...) while((s32[]{:T(128)}, f32[12,192]{1,0:T(8,128)S(1)}, ...), condition=%wide.region_7.8_spmd.clone, body=%wide.region_4.7_spmd.clone.sunk | while | flops 4976258 | bytes 400221 | solution.py:71
  70.5 2.0 gather_fusion.2
  73.0 15.2 %all-gather.9.cloned.1.call-done = bf16[768,768]{1,0:T(8,128)(2,1)} async-done(((bf16[96,768]{1,0:T(8,128)(2,1)}), bf16[768,768]{1,0:T(8,128)(2,1)}) %all-gather.9.cloned.1.call-update) | async-done | bytes 1179664 | tf_op jit(solution)/shard_map/all_gather | solution.py:38
  89.9 24.0 %all-gather.11.cloned.1.call-done = bf16[768,768]{1,0:T(8,128)(2,1)} async-done(((bf16[96,768]{1,0:T(8,128)(2,1)}), bf16[768,768]{1,0:T(8,128)(2,1)}) %all-gather.11.cloned.1.call-update) | async-done | bytes 1179664 | tf_op jit(solution)/shard_map/all_gather | solution.py:39
  118.9 3.9 %gather_fusion = bf16[320,4,768]{2,1,0:T(4,128)(2,1)S(1)} fusion(bf16[193,4,768]{2,1,0:T(4,128)(2,1)S(1)} %concatenate.16.clone, s32[1024]{0:T(1024)S(1)} %pad_clamp_fusion.1), kind=kCustom, calls=%fused_computation | custom fusion | bytes 3933440 | tf_op jit(solution)/shard_map/jit(_take)/gather | solution.py:86
  122.9 3.3 %all-to-all-start.2 = ((f32[8,1,960]{2,1,0:T(1,128)}), f32[8,1,960]{2,1,0:T(1,128)S(1)}, u32[]{:S(2)}, u32[]{:S(2)}) async-start(f32[8,1,960]{2,1,0:T(1,128)} %reshape.247), calls=%async_computation.2 | async-start | bytes 65536 | tf_op jit(solution)/shard_map/all_to_all | solution.py:102
  126.2 2.1 select_convert_fusion
  128.3 2.6 all-to-all-done.2
  131.0 3.8 %all-to-all-start = ((bf16[8,2,20,4,768]{4,3,2,1,0:T(4,128)(2,1)}), bf16[8,2,20,4,768]{4,3,2,1,0:T(4,128)(2,1)S(1)}, u32[]{:S(2)}, u32[]{:S(2)}) async-start(bf16[8,2,20,4,768]{4,3,2,1,0:T(4,128)(2,1)} %select_convert_fusion), calls=%async_computation | async-start | bytes 3932160 | tf_op jit(solution)/shard_map/all_to_all | solution.py:99
  138.6 21.1 %all-to-all-done = bf16[8,2,20,4,768]{4,3,2,1,0:T(4,128)(2,1)S(1)} async-done(((bf16[8,2,20,4,768]{4,3,2,1,0:T(4,128)(2,1)}), bf16[8,2,20,4,768]{4,3,2,1,0:T(4,128)(2,1)S(1)}, u32[]{:S(2)}, u32[]{:S(2)}) %all-to-all-start) | async-done | bytes 1966112 | tf_op jit(solution)/shard_map/all_to_all | solution.py:99
  159.7 2.0 copy.124
  161.7 11.5 %while.42 = (s32[]{:T(128)}, bf16[2,160,768]{2,1,0:T(8,128)(2,1)}, bf16[2,160,768]{2,1,0:T(8,128)(2,1)}, f32[2,160,12]{1,2,0:T(8,128)S(1)}, bf16[2,160,4,768]{3,...) while((s32[]{:T(128)}, bf16[2,160,768]{2,1,0:T(8,128)(2,1)}, ...), condition=%wide.region_11.12_spmd.clone, body=%wide.region_8.11_spmd.clone.sunk | while | flops 121049760 | bytes 14496293 | solution.py:134
  174.2 3.3 %all-to-all-start.3 = ((f32[8,1,480]{2,1,0:T(1,128)}), f32[8,1,480]{2,1,0:T(1,128)S(1)}, u32[]{:S(2)}, u32[]{:S(2)}) async-start(f32[8,1,480]{2,1,0:T(1,128)} %reshape.249), calls=%async_computation.3 | async-start | bytes 32768 | tf_op jit(solution)/shard_map/all_to_all | solution.py:141
  178.9 2.0 copy.147
  182.3 4.2 %all-to-all-start.4 = ((bf16[1,2,160,2,768]{4,3,1,0,2:T(2,128)(2,1)}), bf16[1,2,160,2,768]{4,3,1,0,2:T(2,128)(2,1)}, u32[]{:S(2)}, u32[]{:S(2)}) async-start(bf16[1,2,160,2,768]{4,3,1,0,2:T(2,128)(2,1)} %copy.147), calls=%async_computation.4 | async-start | bytes 1966080 | tf_op jit(solution)/shard_map/all_to_all | solution.py:138
  189.1 42.2 %while.43 = (s32[]{:T(128)}, f32[12,192,64]{1,2,0:T(8,128)}, bf16[12,192,64]{1,2,0:T(8,128)(2,1)S(1)}, bf16[12,192,64]{2,1,0:T(8,128)(2,1)}, bf16[12,192,64]{2,1...) while((s32[]{:T(128)}, f32[12,192,64]{1,2,0:T(8,128)}, ...), condition=%wide.region_13.14_spmd.clone, body=%wide.region_12.13_spmd.clone.sunk | while | flops 14376962 | bytes 546345 | solution.py:154
  235.4 3.1 gather_fusion.4
  241.5 2.4 copy.157
  245.4 36.4 %reduce-scatter.4.cloned.1.call-done = bf16[96,768]{1,0:T(8,128)(2,1)} async-done(((bf16[768,768]{1,0:T(8,128)(2,1)}), bf16[96,768]{1,0:T(8,128)(2,1)}) %reduce-scatter.4.cloned.1.call-update) | async-done | bytes 147472
  284.7 34.9 %all-reduce.5.cloned.1.call-done = bf16[96,768]{0,1:T(8,128)(2,1)} async-done(((bf16[96,768]{0,1:T(8,128)(2,1)}), bf16[96,768]{0,1:T(8,128)(2,1)}) %all-reduce.5.cloned.1.call-update) | async-done | bytes 147472 | tf_op jit(solution)/shard_map/psum | solution.py:174
  (245 shorter events, 101.3 us)
Async XLA Ops:
  7.2 29.4 %copy-start = (bf16[1,192,768]{2,1,0:T(8,128)(2,1)S(1)}, bf16[1,192,768]{2,1,0:T(8,128)(2,1)}, u32[]{:S(2)}) copy-start(bf16[1,192,768]{2,1,0:T(8,128)(2,1)} %param.14) | copy-start | bytes 884740
  7.2 29.4 %all-gather.5.cloned.1.call-start = ((), (), s32[]{:S(2)}) async-start(), calls=%async_computation.6 | async-start | bytes 1327104 | tf_op jit(solution)/shard_map/all_gather | solution.py:36
  7.9 54.5 %all-gather.7.cloned.1.call-start = ((), (), s32[]{:S(2)}) async-start(), calls=%async_computation.7 | async-start | bytes 1327104 | tf_op jit(solution)/shard_map/all_gather | solution.py:37
  8.7 79.6 %all-gather.9.cloned.1.call-start = ((), (), s32[]{:S(2)}) async-start(), calls=%async_computation.8 | async-start | bytes 1327104 | tf_op jit(solution)/shard_map/all_gather | solution.py:38
  17.6 105.2 %all-to-all-start.1 = ((s32[8,2,20]{2,1,0:T(2,128)}), s32[8,2,20]{2,1,0:T(2,128)S(1)}, u32[]{:S(2)}, u32[]{:S(2)}) async-start(s32[8,2,20]{2,1,0:T(2,128)} %broadcast_select_fusion.2), calls=%async_computation.1 | async-start | bytes 16384 | tf_op jit(solution)/shard_map/all_to_all | solution.py:103
  22.8 91.1 %all-gather.11.cloned.1.call-start = ((), (), s32[]{:S(2)}) async-start(), calls=%async_computation.9 | async-start | bytes 1327104 | tf_op jit(solution)/shard_map/all_gather | solution.py:39
  69.4 0.8 copy-start.6
  69.4 3.1 copy-start.7
  70.3 43.6 %copy-start.9 = (bf16[1,192,768]{2,1,0:T(8,128)(2,1)S(1)}, bf16[1,192,768]{2,1,0:T(8,128)(2,1)}, u32[]{:S(2)}) copy-start(bf16[1,192,768]{2,1,0:T(8,128)(2,1)} %param.15) | copy-start | bytes 884740
  89.9 26.7 %copy-start.2 = (bf16[192,768]{1,0:T(8,128)(2,1)}, bf16[192,768]{1,0:T(8,128)(2,1)S(1)}, u32[]{:S(2)}) copy-start(bf16[192,768]{1,0:T(8,128)(2,1)S(1)} %convolution_convert_fusion.4) | copy-start | bytes 884740
  115.7 0.7 copy-start.4
  122.9 8.1 %all-to-all-start.2 = ((f32[8,1,960]{2,1,0:T(1,128)}), f32[8,1,960]{2,1,0:T(1,128)S(1)}, u32[]{:S(2)}, u32[]{:S(2)}) async-start(f32[8,1,960]{2,1,0:T(1,128)} %reshape.247), calls=%async_computation.2 | async-start | bytes 65536 | tf_op jit(solution)/shard_map/all_to_all | solution.py:102
  128.3 6.5 %copy-start.10 = (s32[1,192,1]{1,2,0:T(1,128)S(1)}, s32[1,192,1]{1,2,0:T(1,128)}, u32[]{:S(2)}) copy-start(s32[1,192,1]{1,2,0:T(1,128)} %param.16) | copy-start | bytes 2308
  128.3 6.6 %copy-start.5 = (bf16[192,768]{1,0:T(8,128)(2,1)S(1)}, bf16[192,768]{1,0:T(8,128)(2,1)}, u32[]{:S(2)}) copy-start(bf16[192,768]{1,0:T(8,128)(2,1)} %copy-done.4) | copy-start | bytes 884740
  128.3 7.5 %copy-start.3 = (bf16[192,768]{1,0:T(8,128)(2,1)S(1)}, bf16[192,768]{1,0:T(8,128)(2,1)}, u32[]{:S(2)}) copy-start(bf16[192,768]{1,0:T(8,128)(2,1)} %copy-done.2) | copy-start | bytes 884740
  131.0 28.7 %all-to-all-start = ((bf16[8,2,20,4,768]{4,3,2,1,0:T(4,128)(2,1)}), bf16[8,2,20,4,768]{4,3,2,1,0:T(4,128)(2,1)S(1)}, u32[]{:S(2)}, u32[]{:S(2)}) async-start(bf16[8,2,20,4,768]{4,3,2,1,0:T(4,128)(2,1)} %select_convert_fusion), calls=%async_computation | async-start | bytes 3932160 | tf_op jit(solution)/shard_map/all_to_all | solution.py:99
  174.2 8.0 %all-to-all-start.3 = ((f32[8,1,480]{2,1,0:T(1,128)}), f32[8,1,480]{2,1,0:T(1,128)S(1)}, u32[]{:S(2)}, u32[]{:S(2)}) async-start(f32[8,1,480]{2,1,0:T(1,128)} %reshape.249), calls=%async_computation.3 | async-start | bytes 32768 | tf_op jit(solution)/shard_map/all_to_all | solution.py:141
  180.9 8.3 %copy-start.8 = (bf16[12,192,64]{1,2,0:T(8,128)(2,1)S(1)}, bf16[12,192,64]{1,2,0:T(8,128)(2,1)}, u32[]{:S(2)}) copy-start(bf16[12,192,64]{1,2,0:T(8,128)(2,1)} %custom-call.16) | copy-start | bytes 884740
  182.3 49.6 %all-to-all-start.4 = ((bf16[1,2,160,2,768]{4,3,1,0,2:T(2,128)(2,1)}), bf16[1,2,160,2,768]{4,3,1,0,2:T(2,128)(2,1)}, u32[]{:S(2)}, u32[]{:S(2)}) async-start(bf16[1,2,160,2,768]{4,3,1,0,2:T(2,128)(2,1)} %copy.147), calls=%async_computation.4 | async-start | bytes 1966080 | tf_op jit(solution)/shard_map/all_to_all | solution.py:138
  186.5 95.3 %reduce-scatter.4.cloned.1.call-start = ((), (), s32[]{:S(2)}) async-start(), calls=%async_computation.11 | async-start | bytes 1327104
  243.8 39.7 %copy-start.1 = (bf16[768,768]{1,0:T(8,128)(2,1)S(1)}, bf16[768,768]{1,0:T(8,128)(2,1)}, u32[]{:S(2)}) copy-start(bf16[768,768]{1,0:T(8,128)(2,1)} %all-gather.11.cloned.1.call-done) | copy-start | bytes 3538948
  243.9 75.7 %all-reduce.5.cloned.1.call-start = ((), (), s32[]{:S(2)}) async-start(), calls=%async_computation.10 | async-start | bytes 393216 | tf_op jit(solution)/shard_map/psum | solution.py:174
Sparse Core Ops, SparseCore 0:
  9.9 26.6 all-gather.4
  38.4 23.9 all-gather.6
  64.3 23.9 all-gather.8
  90.0 23.9 all-gather.10
  244.0 37.7 reduce-scatter.3
  284.5 34.9 all-reduce.4
where the time goes:
time: 331 us; the launch traced here: 328 us
  waiting for transfers between devices  175 us (53%)
  matrix products  57.6 us (17%)
  local copies, waits for them, and re-layouts  47.3 us (14%)
  starting transfers between devices  20.3 us (6%)
  between operations  15.3 us (5%)
  other arithmetic  11.8 us (4%)
    unnamed x7, waiting for transfers between devices  39 us
    psum x1, waiting for transfers between devices, local(): lax.psum(grad_part.astype(jnp.bfloat16), 'dp').astype(jnp.float32)  34.9 us
    all_gather x1, waiting for transfers between devices, local(): lax.all_gather(w_out, 'seq', axis=0, tiled=True)  24 us
    all_gather x1, waiting for transfers between devices, local(): lax.all_gather(w_key, 'seq', axis=0, tiled=True)  23.7 us
    all_to_all x1, waiting for transfers between devices, local(): lax.all_to_all(send_bulk.astype(jnp.float32), 'seq', split_axis=0, concat...  21.1 us
    dot_general x12, matrix products, local_apply(): near_out = jnp.dot(weights, value_one, preferred_element_type=jnp.float32)  18.6 us
    dot_general x25, matrix products, contract_last(): lax.dot_general(left, right, (((1,), (1,)), ((), ())), preferred_element_...  17.2 us
    all_gather x1, waiting for transfers between devices, local(): lax.all_gather(w_value, 'seq', axis=0, tiled=True)  15.2 us
  transfers between devices with their start and end apart: 11, of which 9 were waited for; matrix products, arithmetic and copies ran while one was open for 26% of the time, Pallas kernels for 0%

commit v1 on v0

--- a/solution.py
+++ b/solution.py
@@ -32,9 +32,47 @@
     capacity = 5 * rows // (3 * segments)
     slots = segments * capacity
     per_segment = seq_count * capacity
+
+    def plan_digits(local_block):
+        device_axis = "seq"
+        all_rows = jax.lax.psum(1, axis_name=device_axis)
+        arr_now, block_out, clean = (
+            all_rows,
+            jax.lax.axis_index(device_axis),
+            local_block.shape[0],
+        )
+        carry_in = jnp.zeros(
+            [
+                hop_no * arr_now if dev_j == 0 else hop_no
+                for dev_j, hop_no in enumerate(local_block.shape)
+            ],
+            local_block.dtype,
+        )
+        mat_out = g_now = local_block
+        spare = lax.dynamic_update_slice_in_dim(carry_in, local_block, block_out * clean, axis=0)
+        for k in range(1, arr_now // 2 + 1):
+            mat_out = jax.lax.ppermute(
+                mat_out,
+                axis_name=device_axis,
+                perm=[(dev_j, (dev_j + 1) % arr_now) for dev_j in range(arr_now)],
+            )
+            spare = lax.dynamic_update_slice_in_dim(
+                spare, mat_out, (block_out - k) % arr_now * clean, axis=0
+            )
+            if 2 * k < arr_now:
+                g_now = jax.lax.ppermute(
+                    g_now,
+                    device_axis,
+                    perm=[(dev_j, (dev_j - 1) % arr_now) for dev_j in range(arr_now)],
+                )
+                spare = lax.dynamic_update_slice_in_dim(
+                    spare, g_now, (block_out + k) % arr_now * clean, axis=0
+                )
+        return spare
+
     full_query, full_key, full_value, full_out = (
         lax.all_gather(w_query, "seq", axis=0, tiled=True),
-        lax.all_gather(w_key, "seq", axis=0, tiled=True),
+        plan_digits(w_key),
         lax.all_gather(w_value, "seq", axis=0, tiled=True),
         lax.all_gather(w_out, "seq", axis=0, tiled=True),
     )

time: 331 us -> 307 us (0.927)
  waiting for transfers between devices: 175 us -> 145 us
  starting transfers between devices: 20.3 us -> 27.7 us
    all_gather x1 -> x0, waiting for transfers between devices: 23.7 us -> none  [local(): lax.all_gather(w_key, 'seq', axis=0, tiled=True)]
    ppermute x0 -> x7, waiting for transfers between devices: none -> 13.9 us  [the longest x4 13.2 us: plan_digits(): jax.lax.ppermute(mat_out, axis_name=device_axis, perm=[(dev_j, (dev_j + 1...]
    all_gather x1, waiting for transfers between devices: 13.1 us -> 0.02 us  [local(): lax.all_gather(w_query, 'seq', axis=0, tiled=True)]
    ppermute x0 -> x7, starting transfers between devices: none -> 9.05 us  [the longest x3 7.95 us: plan_digits(): jax.lax.ppermute(g_now, device_axis, perm=[(dev_j, (dev_j - 1) % arr_now)...]
    all_gather x1, waiting for transfers between devices: 15.2 us -> 8.85 us  [local(): lax.all_gather(w_value, 'seq', axis=0, tiled=True)]
    unnamed x7 -> x6, waiting for transfers between devices: 39 us -> 37.9 us
    unnamed x36 -> x38, local copies, waits for them, and re-layouts: 11.5 us -> 11.5 us
  transfers between devices with their start and end apart: 11 -> 17, of which waited for: 9 -> 11; matrix products, arithmetic and copies ran while one was open for 26% -> 28% of each run, Pallas kernels for 0% -> 0%
where the time goes in v1:
time: 307 us; the launch traced here: 304 us
  waiting for transfers between devices  145 us (47%)
  matrix products  56.5 us (18%)
  local copies, waits for them, and re-layouts  47.5 us (15%)
  starting transfers between devices  27.7 us (9%)
  between operations  15.2 us (5%)
  other arithmetic  11.8 us (4%)
    unnamed x6, waiting for transfers between devices  37.9 us
    psum x1, waiting for transfers between devices, local(): lax.psum(grad_part.astype(jnp.bfloat16), 'dp').astype(jnp.float32)  34.9 us
    all_gather x1, waiting for transfers between devices, local(): lax.all_gather(w_out, 'seq', axis=0, tiled=True)  24.1 us
    all_to_all x1, waiting for transfers between devices, local(): lax.all_to_all(send_bulk.astype(jnp.float32), 'seq', split_axis=0, concat...  21.1 us
    dot_general x12, matrix products, local_apply(): near_out = jnp.dot(weights, value_one, preferred_element_type=jnp.float32)  18.8 us
    dot_general x25, matrix products, contract_last(): lax.dot_general(left, right, (((1,), (1,)), ((), ())), preferred_element_...  17.2 us
    ppermute x4, waiting for transfers between devices, plan_digits(): jax.lax.ppermute(mat_out, axis_name=device_axis, perm=[(dev_j, (dev_j + 1...  13.2 us
    dot_general x14, matrix products, contract_first(): lax.dot_general(left, right, (((0,), (0,)), ((), ())), preferred_element_...  12.7 us
  transfers between devices with their start and end apart: 17, of which 11 were waited for; matrix products, arithmetic and copies ran while one was open for 28% of the time, Pallas kernels for 0%

profile of v1, /device:TPU:0, one launch (start us, length us, event | category | flops | bytes accessed | tf_op | source)
XLA Modules:
  0.0 304.2 jit_solution(9961045697008506298)
XLA Ops:
  8.5 2.9 collective-permute-start.1
  16.5 2.5 gather_fusion.1
  19.7 3.5 %all-to-all-start.1 = ((s32[8,2,20]{2,1,0:T(2,128)}), s32[8,2,20]{2,1,0:T(2,128)S(1)}, u32[]{:S(2)}, u32[]{:S(2)}) async-start(s32[8,2,20]{2,1,0:T(2,128)} %broadcast_select_fusion.2), calls=%async_computation.1 | async-start | bytes 16384 | tf_op jit(solution)/shard_map/all_to_all | solution.py:141
  24.8 2.2 collective-permute-start.3
  27.1 2.7 collective-permute-done.2
  30.6 2.8 collective-permute-start.5
  33.4 5.1 %collective-permute-done.4 = bf16[96,768]{1,0:T(8,128)(2,1)S(1)} collective-permute-done((bf16[96,768]{1,0:T(8,128)(2,1)S(1)}, bf16[96,768]{1,0:T(8,128)(2,1)S(1)}, u32[]{:S(2)}, u32[]{:S(2)}) %collective-permute-start.4) | collective-permute-done | bytes 147488 | tf_op jit(solution)/shard_map/ppermute | solution.py:54
  38.5 5.4 %collective-permute-done.6 = bf16[96,768]{1,0:T(8,128)(2,1)S(1)} collective-permute-done((bf16[96,768]{1,0:T(8,128)(2,1)S(1)}, bf16[96,768]{1,0:T(8,128)(2,1)S(1)}, u32[]{:S(2)}, u32[]{:S(2)}) %collective-permute-start.6) | collective-permute-done | bytes 147488 | tf_op jit(solution)/shard_map/ppermute | solution.py:54
  47.0 4.8 %while.41 = (s32[]{:T(128)}, f32[12,192]{1,0:T(8,128)S(1)}, f32[12,192]{1,0:T(8,128)S(1)}, bf16[12,192,64]{2,1,0:T(8,128)(2,1)S(1)}, bf16[12,192,64]{2,1,0:T(8,1...) while((s32[]{:T(128)}, f32[12,192]{1,0:T(8,128)S(1)}, ...), condition=%wide.region_7.8_spmd.clone, body=%wide.region_4.7_spmd.clone.sunk | while | flops 4976258 | bytes 400221 | solution.py:109
  55.4 8.8 %all-gather.6.cloned.1.call-done = bf16[768,768]{1,0:T(8,128)(2,1)} async-done(((bf16[96,768]{1,0:T(8,128)(2,1)}), bf16[768,768]{1,0:T(8,128)(2,1)}) %all-gather.6.cloned.1.call-update) | async-done | bytes 1179664 | tf_op jit(solution)/shard_map/all_gather | solution.py:76
  66.0 24.1 %all-gather.8.cloned.1.call-done = bf16[768,768]{1,0:T(8,128)(2,1)} async-done(((bf16[96,768]{1,0:T(8,128)(2,1)}), bf16[768,768]{1,0:T(8,128)(2,1)}) %all-gather.8.cloned.1.call-update) | async-done | bytes 1179664 | tf_op jit(solution)/shard_map/all_gather | solution.py:77
  95.1 3.9 %gather_fusion = bf16[320,4,768]{2,1,0:T(4,128)(2,1)S(1)} fusion(bf16[193,4,768]{2,1,0:T(4,128)(2,1)S(1)} %concatenate.16.clone, s32[1024]{0:T(1024)S(1)} %pad_clamp_fusion.1), kind=kCustom, calls=%fused_computation | custom fusion | bytes 3933440 | tf_op jit(solution)/shard_map/jit(_take)/gather | solution.py:124
  99.1 3.3 %all-to-all-start.2 = ((f32[8,1,960]{2,1,0:T(1,128)}), f32[8,1,960]{2,1,0:T(1,128)S(1)}, u32[]{:S(2)}, u32[]{:S(2)}) async-start(f32[8,1,960]{2,1,0:T(1,128)} %reshape.247), calls=%async_computation.2 | async-start | bytes 65536 | tf_op jit(solution)/shard_map/all_to_all | solution.py:140
  104.5 2.7 all-to-all-done.2
  107.2 3.8 %all-to-all-start = ((bf16[8,2,20,4,768]{4,3,2,1,0:T(4,128)(2,1)}), bf16[8,2,20,4,768]{4,3,2,1,0:T(4,128)(2,1)S(1)}, u32[]{:S(2)}, u32[]{:S(2)}) async-start(bf16[8,2,20,4,768]{4,3,2,1,0:T(4,128)(2,1)} %select_convert_fusion), calls=%async_computation | async-start | bytes 3932160 | tf_op jit(solution)/shard_map/all_to_all | solution.py:137
  114.8 21.1 %all-to-all-done = bf16[8,2,20,4,768]{4,3,2,1,0:T(4,128)(2,1)S(1)} async-done(((bf16[8,2,20,4,768]{4,3,2,1,0:T(4,128)(2,1)}), bf16[8,2,20,4,768]{4,3,2,1,0:T(4,128)(2,1)S(1)}, u32[]{:S(2)}, u32[]{:S(2)}) %all-to-all-start) | async-done | bytes 1966112 | tf_op jit(solution)/shard_map/all_to_all | solution.py:137
  137.9 11.5 %while.42 = (s32[]{:T(128)}, bf16[2,160,768]{2,1,0:T(8,128)(2,1)}, bf16[2,160,768]{2,1,0:T(8,128)(2,1)}, f32[2,160,12]{1,2,0:T(8,128)S(1)}, bf16[2,160,4,768]{3,...) while((s32[]{:T(128)}, bf16[2,160,768]{2,1,0:T(8,128)(2,1)}, ...), condition=%wide.region_11.12_spmd.clone, body=%wide.region_8.11_spmd.clone.sunk | while | flops 121049760 | bytes 14496293 | solution.py:172
  150.4 3.3 %all-to-all-start.3 = ((f32[8,1,480]{2,1,0:T(1,128)}), f32[8,1,480]{2,1,0:T(1,128)S(1)}, u32[]{:S(2)}, u32[]{:S(2)}) async-start(f32[8,1,480]{2,1,0:T(1,128)} %reshape.249), calls=%async_computation.3 | async-start | bytes 32768 | tf_op jit(solution)/shard_map/all_to_all | solution.py:179
  158.4 4.2 %all-to-all-start.4 = ((bf16[1,2,160,2,768]{4,3,1,0,2:T(2,128)(2,1)}), bf16[1,2,160,2,768]{4,3,1,0,2:T(2,128)(2,1)}, u32[]{:S(2)}, u32[]{:S(2)}) async-start(bf16[1,2,160,2,768]{4,3,1,0,2:T(2,128)(2,1)} %copy.147), calls=%async_computation.4 | async-start | bytes 1966080 | tf_op jit(solution)/shard_map/all_to_all | solution.py:176
  165.3 42.4 %while.43 = (s32[]{:T(128)}, f32[12,192,64]{1,2,0:T(8,128)}, bf16[12,192,64]{1,2,0:T(8,128)(2,1)S(1)}, bf16[12,192,64]{2,1,0:T(8,128)(2,1)}, bf16[12,192,64]{2,1...) while((s32[]{:T(128)}, f32[12,192,64]{1,2,0:T(8,128)}, ...), condition=%wide.region_13.14_spmd.clone, body=%wide.region_12.13_spmd.clone.sunk | while | flops 14376962 | bytes 546345 | solution.py:192
  211.7 3.1 %gather_fusion.4 = bf16[192,2,768]{2,1,0:T(2,128)(2,1)S(1)} fusion(bf16[320,2,768]{2,1,0:T(2,128)(2,1)} %bitcast.319, s32[1024]{0:T(1024)S(1)} %pad_clamp_fusion), kind=kCustom, calls=%fused_computation.4 | custom fusion | bytes 1180416 | tf_op jit(solution)/shard_map/jit(_take)/gather | solution.py:181
  217.8 2.4 copy.157
  221.7 36.4 %reduce-scatter.4.cloned.1.call-done = bf16[96,768]{1,0:T(8,128)(2,1)} async-done(((bf16[768,768]{1,0:T(8,128)(2,1)}), bf16[96,768]{1,0:T(8,128)(2,1)}) %reduce-scatter.4.cloned.1.call-update) | async-done | bytes 147472
  261.1 34.9 %all-reduce.5.cloned.1.call-done = bf16[96,768]{0,1:T(8,128)(2,1)} async-done(((bf16[96,768]{0,1:T(8,128)(2,1)}), bf16[96,768]{0,1:T(8,128)(2,1)}) %all-reduce.5.cloned.1.call-update) | async-done | bytes 147472 | tf_op jit(solution)/shard_map/psum | solution.py:212
  (267 shorter events, 109.1 us)
Async XLA Ops:
  7.2 36.8 %copy-start = (bf16[1,192,768]{2,1,0:T(8,128)(2,1)S(1)}, bf16[1,192,768]{2,1,0:T(8,128)(2,1)}, u32[]{:S(2)}) copy-start(bf16[1,192,768]{2,1,0:T(8,128)(2,1)} %param.14) | copy-start | bytes 884740
  7.2 37.7 %all-gather.4.cloned.1.call-start = ((), (), s32[]{:S(2)}) async-start(), calls=%async_computation.6 | async-start | bytes 1327104 | tf_op jit(solution)/shard_map/all_gather | solution.py:74
  7.9 56.3 %all-gather.6.cloned.1.call-start = ((), (), s32[]{:S(2)}) async-start(), calls=%async_computation.7 | async-start | bytes 1327104 | tf_op jit(solution)/shard_map/all_gather | solution.py:76
  8.0 16.3 %collective-permute-start = (bf16[96,768]{1,0:T(8,128)(2,1)}, bf16[96,768]{1,0:T(8,128)(2,1)S(1)}, u32[]{:S(2)}, u32[]{:S(2)}) collective-permute-start(bf16[96,768]{1,0:T(8,128)(2,1)} %param.19), channel_id=1, source_target_pairs={{0,1},{1,2},{2,3},{3,4},{4,5},{5,6},{6,7},{7,0},{8,9},{9,10},{10,1... | collective-permute-start | bytes 442376 | tf_op jit(solution)/shard_map/ppermute | solution.py:54
  8.5 16.3 %collective-permute-start.1 = (bf16[96,768]{1,0:T(8,128)(2,1)}, bf16[96,768]{1,0:T(8,128)(2,1)S(1)}, u32[]{:S(2)}, u32[]{:S(2)}) collective-permute-start(bf16[96,768]{1,0:T(8,128)(2,1)} %param.19), channel_id=1, source_target_pairs={{0,7},{1,0},{2,1},{3,2},{4,3},{5,4},{6,5},{7,6},{8,15},{9,8},{10,9... | collective-permute-start | bytes 442376 | tf_op jit(solution)/shard_map/ppermute | solution.py:63
  19.7 79.3 %all-to-all-start.1 = ((s32[8,2,20]{2,1,0:T(2,128)}), s32[8,2,20]{2,1,0:T(2,128)S(1)}, u32[]{:S(2)}, u32[]{:S(2)}) async-start(s32[8,2,20]{2,1,0:T(2,128)} %broadcast_select_fusion.2), calls=%async_computation.1 | async-start | bytes 16384 | tf_op jit(solution)/shard_map/all_to_all | solution.py:141
  23.2 66.9 %all-gather.8.cloned.1.call-start = ((), (), s32[]{:S(2)}) async-start(), calls=%async_computation.8 | async-start | bytes 1327104 | tf_op jit(solution)/shard_map/all_gather | solution.py:77
  24.3 5.5 %collective-permute-start.2 = (bf16[96,768]{1,0:T(8,128)(2,1)S(1)}, bf16[96,768]{1,0:T(8,128)(2,1)S(1)}, u32[]{:S(2)}, u32[]{:S(2)}) collective-permute-start(bf16[96,768]{1,0:T(8,128)(2,1)S(1)} %collective-permute-done), channel_id=1, source_target_pairs={{0,1},{1,2},{2,3},{3,4},{4,5},{5,6},{6,7},{7,0},{8,9},{9,10},{10,1... | collective-permute-start | bytes 442376 | tf_op jit(solution)/shard_map/ppermute | solution.py:54
  24.8 5.7 %collective-permute-start.3 = (bf16[96,768]{1,0:T(8,128)(2,1)S(1)}, bf16[96,768]{1,0:T(8,128)(2,1)S(1)}, u32[]{:S(2)}, u32[]{:S(2)}) collective-permute-start(bf16[96,768]{1,0:T(8,128)(2,1)S(1)} %collective-permute-done.1), channel_id=1, source_target_pairs={{0,7},{1,0},{2,1},{3,2},{4,3},{5,4},{6,5},{7,6},{8,15},{9,8},{10,9... | collective-permute-start | bytes 442376 | tf_op jit(solution)/shard_map/ppermute | solution.py:63
  29.8 8.6 %collective-permute-start.4 = (bf16[96,768]{1,0:T(8,128)(2,1)S(1)}, bf16[96,768]{1,0:T(8,128)(2,1)S(1)}, u32[]{:S(2)}, u32[]{:S(2)}) collective-permute-start(bf16[96,768]{1,0:T(8,128)(2,1)S(1)} %collective-permute-done.2), channel_id=1, source_target_pairs={{0,1},{1,2},{2,3},{3,4},{4,5},{5,6},{6,7},{7,0},{8,9},{9,10},{10,1... | collective-permute-start | bytes 442376 | tf_op jit(solution)/shard_map/ppermute | solution.py:54
  30.6 7.9 %collective-permute-start.5 = (bf16[96,768]{1,0:T(8,128)(2,1)S(1)}, bf16[96,768]{1,0:T(8,128)(2,1)S(1)}, u32[]{:S(2)}, u32[]{:S(2)}) collective-permute-start(bf16[96,768]{1,0:T(8,128)(2,1)S(1)} %collective-permute-done.3), channel_id=1, source_target_pairs={{0,7},{1,0},{2,1},{3,2},{4,3},{5,4},{6,5},{7,6},{8,15},{9,8},{10,9... | collective-permute-start | bytes 442376 | tf_op jit(solution)/shard_map/ppermute | solution.py:63
  38.5 5.5 %collective-permute-start.6 = (bf16[96,768]{1,0:T(8,128)(2,1)S(1)}, bf16[96,768]{1,0:T(8,128)(2,1)S(1)}, u32[]{:S(2)}, u32[]{:S(2)}) collective-permute-start(bf16[96,768]{1,0:T(8,128)(2,1)S(1)} %collective-permute-done.4), channel_id=1, source_target_pairs={{0,1},{1,2},{2,3},{3,4},{4,5},{5,6},{6,7},{7,0},{8,9},{9,10},{10,1... | collective-permute-start | bytes 442376 | tf_op jit(solution)/shard_map/ppermute | solution.py:54
  55.3 34.8 %copy-start.9 = (bf16[1,192,768]{2,1,0:T(8,128)(2,1)S(1)}, bf16[1,192,768]{2,1,0:T(8,128)(2,1)}, u32[]{:S(2)}) copy-start(bf16[1,192,768]{2,1,0:T(8,128)(2,1)} %param.15) | copy-start | bytes 884740
  65.9 26.9 %copy-start.2 = (bf16[192,768]{1,0:T(8,128)(2,1)}, bf16[192,768]{1,0:T(8,128)(2,1)S(1)}, u32[]{:S(2)}) copy-start(bf16[192,768]{1,0:T(8,128)(2,1)S(1)} %convolution_convert_fusion.5) | copy-start | bytes 884740
  99.1 8.1 %all-to-all-start.2 = ((f32[8,1,960]{2,1,0:T(1,128)}), f32[8,1,960]{2,1,0:T(1,128)S(1)}, u32[]{:S(2)}, u32[]{:S(2)}) async-start(f32[8,1,960]{2,1,0:T(1,128)} %reshape.247), calls=%async_computation.2 | async-start | bytes 65536 | tf_op jit(solution)/shard_map/all_to_all | solution.py:140
  104.5 6.5 %copy-start.11 = (s32[1,192,1]{1,2,0:T(1,128)S(1)}, s32[1,192,1]{1,2,0:T(1,128)}, u32[]{:S(2)}) copy-start(s32[1,192,1]{1,2,0:T(1,128)} %param.16) | copy-start | bytes 2308
  104.5 6.6 %copy-start.5 = (bf16[192,768]{1,0:T(8,128)(2,1)S(1)}, bf16[192,768]{1,0:T(8,128)(2,1)}, u32[]{:S(2)}) copy-start(bf16[192,768]{1,0:T(8,128)(2,1)} %copy-done.4) | copy-start | bytes 884740
  104.5 7.6 %copy-start.3 = (bf16[192,768]{1,0:T(8,128)(2,1)S(1)}, bf16[192,768]{1,0:T(8,128)(2,1)}, u32[]{:S(2)}) copy-start(bf16[192,768]{1,0:T(8,128)(2,1)} %copy-done.2) | copy-start | bytes 884740
  107.2 28.7 %all-to-all-start = ((bf16[8,2,20,4,768]{4,3,2,1,0:T(4,128)(2,1)}), bf16[8,2,20,4,768]{4,3,2,1,0:T(4,128)(2,1)S(1)}, u32[]{:S(2)}, u32[]{:S(2)}) async-start(bf16[8,2,20,4,768]{4,3,2,1,0:T(4,128)(2,1)} %select_convert_fusion), calls=%async_computation | async-start | bytes 3932160 | tf_op jit(solution)/shard_map/all_to_all | solution.py:137
  150.4 8.0 %all-to-all-start.3 = ((f32[8,1,480]{2,1,0:T(1,128)}), f32[8,1,480]{2,1,0:T(1,128)S(1)}, u32[]{:S(2)}, u32[]{:S(2)}) async-start(f32[8,1,480]{2,1,0:T(1,128)} %reshape.249), calls=%async_computation.3 | async-start | bytes 32768 | tf_op jit(solution)/shard_map/all_to_all | solution.py:179
  158.4 49.8 %all-to-all-start.4 = ((bf16[1,2,160,2,768]{4,3,1,0,2:T(2,128)(2,1)}), bf16[1,2,160,2,768]{4,3,1,0,2:T(2,128)(2,1)}, u32[]{:S(2)}, u32[]{:S(2)}) async-start(bf16[1,2,160,2,768]{4,3,1,0,2:T(2,128)(2,1)} %copy.147), calls=%async_computation.4 | async-start | bytes 1966080 | tf_op jit(solution)/shard_map/all_to_all | solution.py:176
  162.7 95.5 %reduce-scatter.4.cloned.1.call-start = ((), (), s32[]{:S(2)}) async-start(), calls=%async_computation.10 | async-start | bytes 1327104
  220.2 39.7 %copy-start.1 = (bf16[768,768]{1,0:T(8,128)(2,1)S(1)}, bf16[768,768]{1,0:T(8,128)(2,1)}, u32[]{:S(2)}) copy-start(bf16[768,768]{1,0:T(8,128)(2,1)} %all-gather.8.cloned.1.call-done) | copy-start | bytes 3538948
  220.2 75.7 %all-reduce.5.cloned.1.call-start = ((), (), s32[]{:S(2)}) async-start(), calls=%async_computation.9 | async-start | bytes 393216 | tf_op jit(solution)/shard_map/psum | solution.py:212
  (5 other events, 12.5 us)
Sparse Core Ops, SparseCore 0:
  9.9 27.3 all-gather.3
  39.1 25.0 all-gather.5
  66.2 23.9 all-gather.7
  220.3 37.8 reduce-scatter.3
  260.9 34.9 all-reduce.4
